TPU v7x, 256 devices: a whole 4x4x8 slice. The times are simulated.
256 devices in a mesh: pts: 64 (over z, x, core), blk: 4 (over y).
Axes of the slice: x: 4, y: 4, z: 8, core: 2. Of those that a mesh axis runs over, the one named last changes fastest.
Arguments:
- points: bfloat16 [2097152, 128], P(('pts', 'blk')), may hold values from -1.5 to 1.5
- targets: float32 [2097152, 64], P(('pts', 'blk')), may hold values from -6 to 6
- coefs: float32 [2097152, 64], P(('pts', 'blk')), may hold values from -0.5 to 0.5
- preds: float32 [2097152, 64], P(('pts', 'blk')), may hold values from -32 to 32
- block_inverse: float32 [2048, 2048], P('blk'), may hold values from -0.2 to 2.2
- block_id: int32 [1], replicated, may hold values from 0 to 1023
Outputs:
- new_coefs: float32 [2097152, 64], P(('pts', 'blk'))
- new_preds: float32 [2097152, 64], P(('pts', 'blk'))
All inputs are finite; a program needn't handle non-finite values.
Results may differ from a plain program's by a relative error of at most 0.0042.
Values may be sent and summed in bfloat16 or wider, within the bound.
A program may use at most 128 MiB of HBM per device.

v0:
```python
import jax
import jax.numpy as jnp
from jax import lax
from jax.sharding import Mesh
from jax.sharding import PartitionSpec as P

PTS_BLK = ("pts_0", "pts_1", "pts_2", "blk")


damping = 1.0
inverse_width = 0.25


def spread(value, axes, root):
    value = jnp.where(lax.axis_index(axes) == root, value, jnp.zeros_like(value))
    for axis in axes:
        value = lax.psum(value, axis)
    return value


def in_blocks(value, dim, length):
    before, after = (value.shape[:dim], value.shape[dim + 1 :])
    return jnp.moveaxis(value.reshape(*before, length, -1, *after), dim, 0)


def sum_at_owner(value, axis, dim):
    pieces = in_blocks(value, dim, lax.axis_size(axis))
    arrived = lax.all_to_all(pieces, axis, split_axis=0, concat_axis=0, tiled=True)
    return arrived.sum(axis=0)


def summed_rows(value, axes, dim):
    far, near = axes
    pieces = in_blocks(value, dim, lax.axis_size(far))
    nearer = sum_at_owner(pieces, near, dim + 1)
    arrived = lax.all_to_all(nearer, far, split_axis=0, concat_axis=0, tiled=True)
    return arrived.sum(axis=0)


def filled_up(lines, length):
    spare = -len(lines) % length
    return jnp.pad(lines, [(0, spare)] + [(0, 0)] * (lines.ndim - 1))


def from_everyone(value, axis):
    copies = jnp.broadcast_to(value, (lax.axis_size(axis), *value.shape))
    return lax.all_to_all(copies, axis, split_axis=0, concat_axis=0, tiled=True)


def laid_out(pieces, dim):
    pieces = jnp.moveaxis(pieces, 0, dim)
    lengths = pieces.shape
    return pieces.reshape(*lengths[:dim], lengths[dim] * lengths[dim + 1], *lengths[dim + 2 :])


def gather_axes(value, axes, dim):
    far, near = axes
    pieces = from_everyone(from_everyone(value, far), near)
    return laid_out(pieces.swapaxes(0, 1).reshape(-1, *value.shape), dim)


def total_of(value, axes):
    lines = value.reshape(-1, value.shape[-1])
    own = summed_rows(filled_up(lines, lax.axis_size(axes[0]) * lax.axis_size(axes[1])), axes, 0)
    whole = gather_axes(own, axes, 0)
    return whole[: len(lines)].reshape(value.shape)


def gathered_copies(value, axis, dim):
    return laid_out(from_everyone(value, axis), dim)


def kernel_rows(centers, others):
    center_wide = centers.astype(jnp.float32)
    other_wide = others.astype(jnp.float32)
    center_squares = jnp.sum(center_wide * center_wide, axis=1)
    point_squares = jnp.sum(other_wide * other_wide, axis=1)
    inner_products = jnp.dot(centers, others.T, preferred_element_type=jnp.float32)
    distance = center_squares[:, None] + point_squares[None, :] - 2.0 * inner_products
    return jnp.exp(-inverse_width * distance).astype(jnp.bfloat16)


def body(points, targets, coefs, preds, block_inverse, block_id):
    shard_rows = points.shape[0]
    block_order = block_inverse.shape[1]
    targets_width = targets.shape[1]
    block_start = block_id[0] * block_order
    owner_index = block_start // shard_rows
    offset = block_start % shard_rows
    is_owner = lax.axis_index(PTS_BLK) == owner_index
    local_centers = lax.dynamic_slice_in_dim(points, offset, block_order, 0)
    centers = spread(local_centers, PTS_BLK, owner_index)
    tile_width = min(512, shard_rows)
    tile_count = shard_rows // tile_width
    point_tiles = points.reshape(tile_count, tile_width, points.shape[1])
    coef_tiles = coefs.astype(jnp.bfloat16).reshape(tile_count, tile_width, targets_width)
    kernel = lax.map(lambda tile_points: kernel_rows(centers, tile_points), point_tiles)
    summed = jnp.einsum("nbs,nsd->bd", kernel, coef_tiles, preferred_element_type=jnp.float32)
    block_coefs = lax.dynamic_slice_in_dim(coefs, offset, block_order, 0)
    own_block = lax.dynamic_slice_in_dim(targets, offset, block_order, 0) - damping * block_coefs
    own_term = jnp.where(is_owner, own_block, 0.0) - summed
    slab_part = sum_at_owner(own_term, "blk", 0)
    slab_part = total_of(slab_part, (("pts_0", "pts_1"), "pts_2"))
    residual = gathered_copies(slab_part, "blk", 0)
    slab_update = jnp.dot(block_inverse, residual, precision=lax.Precision.HIGHEST)
    update = gathered_copies(slab_update, "blk", 0)
    new_coefs = jnp.where(
        is_owner, lax.dynamic_update_slice_in_dim(coefs, block_coefs + update, offset, 0), coefs
    )
    update_half = update.astype(jnp.bfloat16)
    shifts = jnp.einsum("nbs,bd->nsd", kernel, update_half, preferred_element_type=jnp.float32)
    new_preds = preds + shifts.reshape(shard_rows, targets_width)
    return (new_coefs, new_preds)


def solution(mesh):
    split = Mesh(
        mesh.devices.reshape(8, 4, 2, mesh.shape["blk"]), ("pts_0", "pts_1", "pts_2", "blk")
    )
    in_specs = (
        P(PTS_BLK, None),
        P(PTS_BLK, None),
        P(PTS_BLK, None),
        P(PTS_BLK, None),
        P("blk", None),
        P(),
    )
    out_specs = (P(PTS_BLK, None), P(PTS_BLK, None))
    return jax.shard_map(body, mesh=split, in_specs=in_specs, out_specs=out_specs, check_vma=False)
```

profile of v0, /device:TPU:1, one launch (start us, length us, event | category | flops | bytes accessed | tf_op | source)
XLA Modules:
  0.0 446.5 jit_solution(14518260487018970397)
XLA Ops:
  7.2 1.6 copy.69
  9.5 2.0 dynamic-slice_select_fusion
  11.6 73.0 %all-reduce.5.cloned.1.call-done = bf16[2048,128]{1,0:T(8,128)(2,1)} async-done(((bf16[2048,128]{1,0:T(8,128)(2,1)}), bf16[2048,128]{1,0:T(8,128)(2,1)}) %all-reduce.5.cloned.1.call-update) | async-done | bytes 524304 | tf_op jit(solution)/shard_map/psum | solution.py:17
  84.6 51.3 %all-reduce.7.cloned.1.call-done = bf16[2048,128]{1,0:T(8,128)(2,1)} async-done(((bf16[2048,128]{1,0:T(8,128)(2,1)}), bf16[2048,128]{1,0:T(8,128)(2,1)}) %all-reduce.7.cloned.1.call-update) | async-done | bytes 524304 | tf_op jit(solution)/shard_map/psum | solution.py:17
  136.0 35.4 %all-reduce.9.cloned.1.call-done = bf16[2048,128]{1,0:T(8,128)(2,1)} async-done(((bf16[2048,128]{1,0:T(8,128)(2,1)}), bf16[2048,128]{1,0:T(8,128)(2,1)}) %all-reduce.9.cloned.1.call-update) | async-done | bytes 524304 | tf_op jit(solution)/shard_map/psum | solution.py:17
  171.6 48.7 %all-reduce.11.cloned.1.call-done = bf16[2048,128]{1,0:T(8,128)(2,1)} async-done(((bf16[2048,128]{1,0:T(8,128)(2,1)}), bf16[2048,128]{1,0:T(8,128)(2,1)}) %all-reduce.11.cloned.1.call-update) | async-done | bytes 524304 | tf_op jit(solution)/shard_map/psum | solution.py:17
  220.3 96.1 %while.10 = (s32[]{:T(128)}, bf16[16,2048,512]{1,2,0:T(8,128)(2,1)}, bf16[2048,128]{1,0:T(8,128)(2,1)}, bf16[16,512,128]{2,1,0:T(8,128)(2,1)}, s32[]{:T(128)}) while((s32[]{:T(128)}, bf16[16,2048,512]{1,2,0:T(8,128)(2,1)}, bf16[2048,128]{1,0:T(8,128)(2,1)}, bf16[16,512,128]{2,1,0:T(8,128)(2,1)}, s32[]{:T(128)}) %tuple.33), condition=%wide.region_7.8_spmd, body=%wide.region_4.7_spmd.sunk | while | flops 274658816 | bytes 3429441 | solution.py:97
  221.3 1.4 multiply_reduce_fusion.5
  222.7 3.6 fusion.22
  227.4 1.4 multiply_reduce_fusion.5
  228.8 3.5 fusion.22
  233.3 1.4 multiply_reduce_fusion.5
  234.7 3.6 fusion.22
  239.3 1.4 multiply_reduce_fusion.5
  240.7 3.6 fusion.22
  245.3 1.4 multiply_reduce_fusion.5
  246.7 3.6 fusion.22
  251.4 1.4 multiply_reduce_fusion.5
  252.8 3.5 fusion.22
  257.4 1.4 multiply_reduce_fusion.5
  258.8 3.6 fusion.22
  263.4 1.4 multiply_reduce_fusion.5
  264.8 3.6 fusion.22
  269.4 1.4 multiply_reduce_fusion.5
  270.8 3.6 fusion.22
  275.4 1.4 multiply_reduce_fusion.5
  276.8 3.5 fusion.22
  281.4 1.4 multiply_reduce_fusion.5
  282.8 3.5 fusion.22
  287.4 1.4 multiply_reduce_fusion.5
  288.8 3.6 fusion.22
  293.4 1.4 multiply_reduce_fusion.5
  294.8 3.6 fusion.22
  299.4 1.4 multiply_reduce_fusion.5
  300.8 3.5 fusion.22
  305.4 1.4 multiply_reduce_fusion.5
  306.8 3.6 fusion.22
  312.8 3.5 fusion.22
  316.3 14.1 %fusion.8 = f32[2048,64]{0,1:T(8,128)S(1)} fusion(bf16[16,2048,512]{1,2,0:T(8,128)(2,1)} %get-tuple-element.24, bf16[8,16,8,512]{3,2,1,0:T(8,128)(2,1)S(1)} %bitcast.68, f32[8192,64]{0,1:T(8,128)} %param.9, s32[]{:T(128)S(6)} %select_n.44, f32[8192,64]{0,1:T(8,128)S(1)} %copy.69, pred[]{:T(512)S(6)} %eq.6), kind=kOutput, calls=%fused_computation.13 | convolution fusion | flops 2147876864 | bytes 36175876 | tf_op jit(solution)/shard_map/nbs,nsd->bd/dot_general | solution.py:98
  330.5 10.2 %all_to_all.35 = f32[4,512,64]{1,2,0:T(8,128)S(1)} all-to-all(f32[4,512,64]{1,2,0:T(8,128)S(1)} %bitcast.72), channel_id=1, replica_groups=mesh['pts_0'=8,'pts_1'=4,'pts_2'=2,'blk'=4] {'blk'}, dimensions={0} | all-to-all | bytes 1048576 | tf_op jit(solution)/shard_map/all_to_all | solution.py:28
  341.1 7.7 %all_to_all.36 = f32[2,1,16384]{2,1,0:T(1,128)S(1)} all-to-all(f32[2,1,16384]{2,1,0:T(1,128)S(1)} %reshape.32), channel_id=1, replica_groups=mesh['pts_0'=8,'pts_1'=4,'pts_2'=2,'blk'=4] {'pts_2'}, dimensions={0} | all-to-all | bytes 262144 | tf_op jit(solution)/shard_map/all_to_all | solution.py:28
  350.7 18.1 %all_to_all.37 = f32[32,1,512]{2,1,0:T(1,128)S(1)} all-to-all(f32[32,1,512]{2,1,0:T(1,128)S(1)} %reshape.34), channel_id=1, replica_groups=mesh['pts_0'=8,'pts_1'=4,'pts_2'=2,'blk'=4] {'pts_0','pts_1'}, dimensions={0} | all-to-all | bytes 131072 | tf_op jit(solution)/shard_map/all_to_all | solution.py:36
  369.9 12.0 %all_to_all.38 = f32[32,1,512]{2,1,0:T(1,128)S(1)} all-to-all(f32[32,1,512]{2,1,0:T(1,128)S(1)} %reshape.36), channel_id=1, replica_groups=mesh['pts_0'=8,'pts_1'=4,'pts_2'=2,'blk'=4] {'pts_0','pts_1'}, dimensions={0} | all-to-all | bytes 131072 | tf_op jit(solution)/shard_map/all_to_all | solution.py:47
  383.0 6.4 %all_to_all.39 = f32[2,1,16384]{2,1,0:T(1,128)S(1)} all-to-all(f32[2,1,16384]{2,1,0:T(1,128)S(1)} %reshape.38), channel_id=1, replica_groups=mesh['pts_0'=8,'pts_1'=4,'pts_2'=2,'blk'=4] {'pts_2'}, dimensions={0} | all-to-all | bytes 262144 | tf_op jit(solution)/shard_map/all_to_all | solution.py:47
  390.8 11.6 %all_to_all.40 = f32[4,512,64]{1,2,0:T(8,128)S(1)} all-to-all(f32[4,512,64]{1,2,0:T(8,128)S(1)} %broadcast_in_dim.33), channel_id=1, replica_groups=mesh['pts_0'=8,'pts_1'=4,'pts_2'=2,'blk'=4] {'blk'}, dimensions={0} | all-to-all | bytes 1048576 | tf_op jit(solution)/shard_map/all_to_all | solution.py:47
  402.5 6.3 %convolution_bitcast_fusion.1 = f32[512,64]{0,1:T(8,128)S(1)} fusion(f32[2048,64]{0,1:T(8,128)S(1)} %bitcast.71, f32[512,2048]{1,0:T(8,128)} %param.12), kind=kOutput, calls=%fused_computation.14 | convolution fusion | flops 805306368 | bytes 4849664 | tf_op jit(solution)/shard_map/dot_general | solution.py:105
  408.8 10.9 %all_to_all.41 = f32[4,512,64]{1,2,0:T(8,128)S(1)} all-to-all(f32[4,512,64]{1,2,0:T(8,128)S(1)} %broadcast_in_dim.34), channel_id=1, replica_groups=mesh['pts_0'=8,'pts_1'=4,'pts_2'=2,'blk'=4] {'blk'}, dimensions={0} | all-to-all | bytes 1048576 | tf_op jit(solution)/shard_map/all_to_all | solution.py:47
  421.0 19.1 %convolution_add_fusion = f32[8192,64]{0,1:T(8,128)} fusion(f32[8192,64]{0,1:T(8,128)} %param.11, bf16[8192,2048]{1,0:T(8,128)(2,1)} %bitcast.67, bf16[2048,64]{0,1:T(8,128)(2,1)S(1)} %bitcast.75), kind=kOutput, calls=%fused_computation.11 | convolution fusion | flops 2148007936 | bytes 38010880 | tf_op jit(solution)/shard_map/nbs,bd->nsd/dot_general | solution.py:111
  (60 shorter events, 25.5 us)
Async XLA Ops:
  7.2 77.4 %all-reduce.5.cloned.1.call-start = ((), (), s32[]{:S(2)}) async-start(), calls=%async_computation.7 | async-start | bytes 1048576 | tf_op jit(solution)/shard_map/psum | solution.py:17
  11.5 124.4 %all-reduce.7.cloned.1.call-start = ((), (), s32[]{:S(2)}) async-start(), calls=%async_computation.8 | async-start | bytes 1048576 | tf_op jit(solution)/shard_map/psum | solution.py:17
  84.6 86.9 %all-reduce.9.cloned.1.call-start = ((), (), s32[]{:S(2)}) async-start(), calls=%async_computation.9 | async-start | bytes 1048576 | tf_op jit(solution)/shard_map/psum | solution.py:17
  136.0 84.3 %all-reduce.11.cloned.1.call-start = ((), (), s32[]{:S(2)}) async-start(), calls=%async_computation.10 | async-start | bytes 1048576 | tf_op jit(solution)/shard_map/psum | solution.py:17
  420.9 19.1 %copy-start = (f32[8192,64]{0,1:T(8,128)}, f32[8192,64]{0,1:T(8,128)S(1)}, u32[]{:S(2)}) copy-start(f32[8192,64]{0,1:T(8,128)S(1)} %select_n.49) | copy-start | bytes 6291460
Sparse Core Ops, SparseCore 0:
  11.7 72.8 all-reduce.4
  86.9 49.0 all-reduce.6
  138.6 32.8 all-reduce.8
  173.6 46.5 all-reduce.10
where the time goes:
time: 448 us; the launch traced here: 447 us
  waiting for transfers between devices  208 us (46%)
  matrix products  96.4 us (22%)
  blocking collectives  77 us (17%)
  other arithmetic  45.1 us (10%)
  between operations  14.7 us (3%)
  local copies, waits for them, and re-layouts  4.66 us (1%)
    psum x4, waiting for transfers between devices, spread(): value = lax.psum(value, axis)  208 us
    dot_general x16, matrix products, kernel_rows(): jnp.dot(centers, others.T, preferred_element_type=jnp.float32)  56.9 us
    all_to_all x4, blocking collectives, from_everyone(): return lax.all_to_all(copies, axis, split_axis=0, concat_axis=0, tiled=True)  41 us
    reduce_sum x16, other arithmetic, kernel_rows(): center_squares = jnp.sum(center_wide * center_wide, axis=1)  22.2 us
    dot_general x1, matrix products, body(): jnp.einsum('nbs,bd->nsd', kernel, update_half, preferred_element_type=jnp...  19.1 us
    all_to_all x1, blocking collectives, summed_rows(): lax.all_to_all(nearer, far, split_axis=0, concat_axis=0, tiled=True)  18.1 us
    all_to_all x2, blocking collectives, sum_at_owner(): lax.all_to_all(pieces, axis, split_axis=0, concat_axis=0, tiled=True)  17.9 us
    reduce_sum x16, other arithmetic, kernel_rows(): point_squares = jnp.sum(other_wide * other_wide, axis=1)  16.8 us
  transfers between devices with their start and end apart: 4, of which 4 were waited for; matrix products, arithmetic and copies ran while one was open for 0% of the time, Pallas kernels for 0%

commit v1 on v0

v1 whole, which is shorter than its diff:
```python
import jax
import jax.numpy as jnp
from jax import lax
from jax.experimental import pallas as pl
from jax.experimental.pallas import tpu as pltpu
from jax.sharding import Mesh
from jax.sharding import PartitionSpec as P

AXES = ("z", "x", "c", "y")
MESH = pl.DeviceIdType.MESH
F, T, B, R = 128, 64, 2048, 8192
SLAB = 512
NS = B // SLAB
CHUNK = 2048
NCH = R // CHUNK
PIECE = 64
HALF = B // 2
SCALE = 0.5 * 1.4426950408889634
NT = (((1,), (1,)), ((), ()))
NN = (((1,), (0,)), ((), ()))
f32, bf16 = jnp.float32, jnp.bfloat16


def dg(a, b, dims):
    return lax.dot_general(a, b, dims, preferred_element_type=f32)


def rem(a, n):
    return lax.rem(a, jnp.int32(n))


def div(a, n):
    return lax.div(a, jnp.int32(n))


def extra_columns(rows, norm_first):
    wide = rows.astype(f32)
    half_norm = -0.5 * jnp.sum(wide * wide, axis=1, keepdims=True)
    high = half_norm.astype(bf16).astype(f32)
    rest = half_norm - high
    middle = rest.astype(bf16).astype(f32)
    low = rest - middle
    lane = lax.broadcasted_iota(jnp.int32, rows.shape, 1)
    at = 0 if norm_first else 3
    ones_at = 3 - at
    out = jnp.where((lane >= ones_at) & (lane < ones_at + 3), 1.0, 0.0)
    out = jnp.where(lane == at, high, out)
    out = jnp.where(lane == at + 1, middle, out)
    out = jnp.where(lane == at + 2, low, out)
    return out.astype(bf16)


def kernel(
    bid, pts_hbm, tg_hbm, cf_hbm, pr_hbm, inv_hbm, nc_hbm, np_hbm,
    km, xa, ca, w16, cf, pr, stage, ihi, ilo, own,
    cand, crecv, hb, rbuf, pbuf, zbuf, fbuf,
    part, rs, ysend, ybuf, zsend, zsum, upd, ubuf, ub,
    lsem, asend, arecv, bsend, brecv, gsend, grecv, usend, urecv,
):
    z, x, c, y = (lax.axis_index(a) for a in AXES)
    plane = x * 4 + y
    q = x * 2 + c
    block = bid[0]
    quarter = rem(block, 4)
    owner = div(block, 4)
    oy = rem(owner, 4)
    oc = rem(div(owner, 4), 2)
    ox = rem(div(owner, 8), 4)
    oz = div(owner, 32)
    oplane = ox * 4 + oy

    def weight(a, b):
        return (a == b).astype(jnp.int32)

    owns = weight(oz, z) * weight(ox, x) * weight(oc, c) * weight(oy, y)

    def pick(index, n, read):
        value = read(0).astype(f32) * weight(index, 0).astype(f32)
        for i in range(1, n):
            value = value + read(i).astype(f32) * weight(index, i).astype(f32)
        return value

    def remote(src, dst, ssem, rsem, dz, dx, dc, dy):
        return pltpu.make_async_remote_copy(
            src_ref=src, dst_ref=dst, send_sem=ssem, recv_sem=rsem,
            device_id=(dz, dx, dc, dy), device_id_type=MESH)

    def plane_peer(d):
        return rem(x + div(d, 4), 4), rem(y + rem(d, 4), 4)

    def xc_peer(d):
        peer = rem(q + d, 8)
        return peer, div(peer, 2), rem(peer, 2)

    def loop(low, high, fn):
        lax.fori_loop(low, high, lambda i, t: (fn(i), t)[1], 0)

    def wait_bytes(view, sem):
        pltpu.make_async_copy(view, view, sem).wait()

    points_in = pltpu.make_async_copy(pts_hbm, xa.at[:, pl.ds(0, F)], lsem.at[0])
    points_in.start()
    targets_in = pltpu.make_async_copy(tg_hbm, pr, lsem.at[1])
    targets_in.start()
    coefs_in = pltpu.make_async_copy(cf_hbm, cf, lsem.at[2])
    coefs_in.start()

    barrier = pltpu.get_barrier_semaphore()

    def greet(dz, dx, dc, dy):
        pl.semaphore_signal(barrier, inc=1, device_id=(dz, dx, dc, dy), device_id_type=MESH)

    def greet_plane(d):
        px, py = plane_peer(d)
        greet(z, px, c, py)

    loop(1, 16, greet_plane)
    loop(1, 8, lambda d: greet(rem(z + d, 8), x, c, y))
    loop(0, 4, lambda d: greet(z, rem(x + d, 4), 1 - c, y))

    points_in.wait()

    def local_half(half):
        def read(k):
            return xa[pl.ds(pl.multiple_of(k * B + half * HALF, HALF), HALF), pl.ds(0, F)]

        return pick(quarter, 4, read)

    cand[...] = local_half(1 - c).astype(bf16)
    pl.semaphore_wait(barrier, 26)

    swap = remote(cand, crecv, asend.at[0], arecv.at[0], z, x, 1 - c, y)
    swap.start()
    swap.wait()
    hb[...] = pick(weight(oc, c), 2, lambda k: local_half(c) if k else crecv[...]).astype(bf16)

    def scatter(d):
        px, py = plane_peer(d)
        row = pl.multiple_of((px * 4 + py) * PIECE, PIECE)
        remote(hb.at[pl.ds(row, PIECE), :], rbuf.at[plane], asend.at[1], arecv.at[1], z, px, c, py).start()

    loop(1, 16, scatter)
    rbuf[plane] = hb[pl.ds(pl.multiple_of(plane * PIECE, PIECE), PIECE), :]

    def widen_points(i):
        rows = pl.ds(pl.multiple_of(i * 512, 512), 512)
        xa[rows, pl.ds(F, F)] = extra_columns(xa[rows, pl.ds(0, F)], False)

    loop(0, R // 512, widen_points)

    wait_bytes(rbuf.at[pl.ds(0, 15)], arecv.at[1])
    pbuf[...] = pick(oplane, 16, lambda k: rbuf[k]).astype(bf16)
    zbuf[z] = pbuf[...]

    def along_z(d):
        remote(pbuf, zbuf.at[z], asend.at[2], arecv.at[2], rem(z + d, 8), x, c, y).start()

    loop(1, 8, along_z)

    coefs_in.wait()
    targets_in.wait()

    def narrow(i):
        cols = pl.ds(pl.multiple_of(i * 1024, 1024), 1024)
        w16[:, cols] = cf[:, cols].astype(bf16)

    loop(0, R // 1024, narrow)
    own[...] = pick(quarter, 4, lambda k: pr[:, pl.ds(k * B, B)] - cf[:, pl.ds(k * B, B)]) * owns.astype(f32)
    preds_in = pltpu.make_async_copy(pr_hbm, pr, lsem.at[1])
    preds_in.start()

    wait_bytes(zbuf.at[pl.ds(0, 7)], arecv.at[2])
    fbuf[...] = pick(oz, 8, lambda k: zbuf[k]).astype(bf16)
    my_rows = pl.ds(pl.multiple_of(c * HALF + plane * PIECE, PIECE), PIECE)
    ca[my_rows, pl.ds(0, F)] = fbuf[...]

    def gather(d):
        px, py = plane_peer(d)
        remote(fbuf, ca.at[my_rows, pl.ds(0, F)], asend.at[3], arecv.at[3], z, px, c, py).start()

    loop(1, 16, gather)

    def split_inverse(i):
        rows = pl.ds(pl.multiple_of(i * 128, 128), 128)
        load = pltpu.make_async_copy(inv_hbm.at[rows, :], stage, lsem.at[3])
        load.start()
        load.wait()
        value = stage[...]
        high = value.astype(bf16)
        ihi[rows, :] = high
        ilo[rows, :] = (value - high.astype(f32)).astype(bf16)

    loop(0, SLAB // 128, split_inverse)

    wait_bytes(rbuf.at[pl.ds(0, 15)], arecv.at[3])
    half_rows = pl.ds(pl.multiple_of(c * HALF, HALF), HALF)
    share = remote(ca.at[half_rows, pl.ds(0, F)], ca.at[half_rows, pl.ds(0, F)],
                   asend.at[4], arecv.at[4], z, x, 1 - c, y)
    share.start()
    share.wait()

    def widen_centers(i):
        rows = pl.ds(pl.multiple_of(i * 512, 512), 512)
        ca[rows, pl.ds(F, F)] = extra_columns(ca[rows, pl.ds(0, F)], True)

    loop(0, B // 512, widen_centers)

    def slab_work(s):
        cols = pl.ds(s * SLAB, SLAB)
        part[s] = own[:, cols]

        def step(j):
            rows = pl.ds(pl.multiple_of(j * CHUNK, CHUNK), CHUNK)
            exponent = dg(xa[rows, :], ca[cols, :], NT)
            tile = jnp.exp2(exponent * SCALE).astype(bf16)
            km[rows, cols] = tile
            part[s] -= dg(w16[:, rows], tile, NN)

        loop(0, NCH, step)

        def send(d):
            peer, px, pc = xc_peer(d)
            rows = pl.ds(pl.multiple_of(peer * 8, 8), 8)
            remote(part.at[s, rows, :], rs.at[s, q], bsend.at[s, 0], brecv.at[s, 0], z, px, pc, y).start()

        loop(1, 8, send)
        rs[s, q] = part[s, pl.ds(pl.multiple_of(q * 8, 8), 8), :]

    def total(ref, s, n):
        value = ref[s, 0]
        for i in range(1, n):
            value = value + ref[s, i]
        return value

    def over_y(s):
        wait_bytes(rs.at[s, pl.ds(0, 7)], brecv.at[s, 0])
        value = total(rs, s, 8)
        ysend[s] = value
        ybuf[s, y] = value

        def send(d):
            remote(ysend.at[s], ybuf.at[s, y], bsend.at[s, 1], brecv.at[s, 1], z, x, c, rem(y + d, 4)).start()

        loop(1, 4, send)

    def over_z(s):
        wait_bytes(ybuf.at[s, pl.ds(0, 3)], brecv.at[s, 1])
        value = total(ybuf, s, 4)
        zsend[s] = value
        zsum[s, z] = value

        def send(d):
            remote(zsend.at[s], zsum.at[s, z], bsend.at[s, 2], brecv.at[s, 2], rem(z + d, 8), x, c, y).start()

        loop(1, 8, send)

    def apply_inverse(s):
        wait_bytes(zsum.at[s, pl.ds(0, 7)], brecv.at[s, 2])
        residual = total(zsum, s, 8)
        high = residual.astype(bf16).astype(f32)
        both = jnp.concatenate([high, residual - high], axis=0).astype(bf16)
        cols = pl.ds(s * SLAB, SLAB)
        by_high = dg(both, ihi[:, cols], NT)
        by_low = dg(both, ilo[:, cols], NT)
        add = by_high[0:8] + by_high[8:16] + by_low[0:8]
        upd[...] = add if s == 0 else upd[...] + add

    for t in range(NS + 3):
        if t < NS:
            slab_work(t)
        if 0 <= t - 1 < NS:
            over_y(t - 1)
        if 0 <= t - 2 < NS:
            over_z(t - 2)
        if 0 <= t - 3 < NS:
            apply_inverse(t - 3)

    upd_rows = pl.ds(pl.multiple_of(q * 8, 8), 8)
    ubuf[upd_rows, :] = upd[...]

    def gather_update(d):
        peer, px, pc = xc_peer(d)
        remote(upd, ubuf.at[upd_rows, :], gsend.at[0], grecv.at[0], z, px, pc, y).start()

    loop(1, 8, gather_update)
    wait_bytes(ubuf.at[pl.ds(0, 56), :], grecv.at[0])
    ub[y] = ubuf[...].astype(bf16)

    def share_update(d):
        remote(ub.at[y], ub.at[y], usend.at[d], urecv.at[4 - d], z, x, c, rem(y + d, 4)).start()

    loop(1, 4, share_update)
    preds_in.wait()

    outs = []
    for i, d in enumerate((0, 1, 3, 2)):
        slab = rem(y + d, 4)
        if d:
            wait_bytes(ub.at[slab], urecv.at[d])
        if i == 3:
            for s in range(NS):
                for k in range(4):
                    cols = pl.ds(k * B + s * SLAB, SLAB)
                    cf[:, cols] += ub[s].astype(f32) * (owns * weight(quarter, k)).astype(f32)
            coefs_out = pltpu.make_async_copy(cf, nc_hbm, lsem.at[2])
            coefs_out.start()

        def advance(j, slab=slab):
            rows = pl.ds(pl.multiple_of(j * CHUNK, CHUNK), CHUNK)
            cols = pl.ds(pl.multiple_of(slab * SLAB, SLAB), SLAB)
            pr[:, rows] += dg(ub[slab], km[rows, cols], NT)

        loop(0, NCH, advance)
    preds_out = pltpu.make_async_copy(pr, np_hbm, lsem.at[1])
    preds_out.start()

    wait_bytes(rbuf.at[pl.ds(0, 15)], asend.at[1])
    wait_bytes(zbuf.at[pl.ds(0, 7)], asend.at[2])
    wait_bytes(rbuf.at[pl.ds(0, 15)], asend.at[3])
    for s in range(NS):
        wait_bytes(rs.at[s, pl.ds(0, 7)], bsend.at[s, 0])
        wait_bytes(ybuf.at[s, pl.ds(0, 3)], bsend.at[s, 1])
        wait_bytes(zsum.at[s, pl.ds(0, 7)], bsend.at[s, 2])
    wait_bytes(ubuf.at[pl.ds(0, 56), :], gsend.at[0])
    for d in range(1, 4):
        wait_bytes(ub.at[0], usend.at[d])
    coefs_out.wait()
    preds_out.wait()


def body(points, targets, coefs, preds, block_inverse, block_id):
    hbm = pl.BlockSpec(memory_space=pl.ANY)
    V, D = pltpu.VMEM, pltpu.SemaphoreType.DMA
    new_coefs, new_preds = pl.pallas_call(
        kernel,
        name="ridge_step",
        in_specs=[pl.BlockSpec(memory_space=pltpu.SMEM)] + [hbm] * 5,
        out_specs=[hbm, hbm],
        out_shape=[jax.ShapeDtypeStruct((T, R), f32)] * 2,
        scratch_shapes=[
            V((R, B), bf16), V((R, 2 * F), bf16), V((B, 2 * F), bf16), V((T, R), bf16), V((T, R), f32), V((T, R), f32),
            V((128, B), f32), V((SLAB, B), bf16), V((SLAB, B), bf16), V((T, B), f32),
            V((HALF, F), bf16), V((HALF, F), bf16), V((HALF, F), bf16), V((16, PIECE, F), bf16),
            V((PIECE, F), bf16), V((8, PIECE, F), bf16), V((PIECE, F), bf16),
            V((NS, T, SLAB), f32), V((NS, 8, 8, SLAB), f32), V((NS, 8, SLAB), f32), V((NS, 4, 8, SLAB), f32),
            V((NS, 8, SLAB), f32), V((NS, 8, 8, SLAB), f32), V((8, SLAB), f32), V((T, SLAB), f32), V((4, T, SLAB), bf16),
            D((4,)), D((5,)), D((5,)), D((NS, 3)), D((NS, 3)), D((1,)), D((1,)), D((4,)), D((4,)),
        ],
        compiler_params=pltpu.CompilerParams(collective_id=0, has_side_effects=True, vmem_limit_bytes=61 << 20),
    )(block_id, points, targets.T, coefs.T, preds.T, block_inverse)
    return new_coefs.T, new_preds.T


def solution(mesh):
    split = Mesh(mesh.devices.reshape(8, 4, 2, mesh.shape["blk"]), AXES)
    rows = P(AXES, None)
    return jax.shard_map(
        body, mesh=split, in_specs=(rows, rows, rows, rows, P("y", None), P()), out_specs=(rows, rows), check_vma=False)
```

time: 448 us -> 89.9 us (0.20)
  waiting for transfers between devices: 208 us -> 0 us
  matrix products: 96.4 us -> 0 us
  Pallas kernels: 0 us -> 83.8 us
  blocking collectives: 77 us -> 0 us
  other arithmetic: 45.1 us -> 0 us
  between operations: 14.7 us -> 1.3 us
    psum x4 -> x0, waiting for transfers between devices: 208 us -> none  [spread(): value = lax.psum(value, axis)]
    dot_general x19 -> x0, matrix products: 96.4 us -> none  [the longest x16 56.9 us: kernel_rows(): jnp.dot(centers, others.T, preferred_element_type=jnp.float32)]
    pallas_call x0 -> x1, Pallas kernels: none -> 83.8 us  [body(): pl.pallas_call(kernel, name='ridge_step', in_specs=[pl.BlockSpec(memory_s...]
    all_to_all x7 -> x0, blocking collectives: 77 us -> none  [the longest x4 41 us: from_everyone(): return lax.all_to_all(copies, axis, split_axis=0, concat_axis=0, tiled=True)]
    reduce_sum x35 -> x0, other arithmetic: 39 us -> none  [the longest x16 22.2 us: kernel_rows(): center_squares = jnp.sum(center_wide * center_wide, axis=1)]
  transfers between devices with their start and end apart: 4 -> 0, of which waited for: 4 -> 0; matrix products, arithmetic and copies ran while one was open for 0% -> 0% of each run, Pallas kernels for 0% -> 0%
where the time goes in v1:
time: 89.9 us; the launch traced here: 89.6 us
  Pallas kernels  83.8 us (93%)
  local copies, waits for them, and re-layouts  4.53 us (5%)
  between operations  1.3 us (1%)
    pallas_call x1, Pallas kernels, body(): pl.pallas_call(kernel, name='ridge_step', in_specs=[pl.BlockSpec(memory_s...  83.8 us
    unnamed x4, local copies, waits for them, and re-layouts  4.53 us

profile of v1, /device:TPU:1, one launch (start us, length us, event | category | flops | bytes accessed | tf_op | source)
XLA Modules:
  0.0 89.6 jit_solution(1052945778415040028)
XLA Ops:
  1.3 83.8 %ridge_step.1 = (f32[64,8192]{1,0:T(8,128)}, f32[64,8192]{1,0:T(8,128)}) custom-call(s32[1]{0:T(128)S(6)} %copy.10.bid, bf16[8192,128]{1,0:T(8,128)(2,1)} %pts_hbm.1, f32[64,8192]{1,0:T(8,128)} %bitcast.5, f32[64,8192]{1,0:T(8,128)} %bitcast.6, f32[64,8192]{1,0:T(8,128)} %bitcast.7, f32[512,2048]{1,0:T(8,128)} %inv_hbm.1), custom_call_target="tpu_custom_call" | custom-call | tf_op jit(solution)/shard_map/ridge_step/pallas_call | solution.py:334
  85.1 0.0 copy-start
  85.1 3.2 %copy.11 = f32[8192,64]{0,1:T(8,128)} copy(f32[8192,64]{0,1:T(8,128)} %bitcast.9) | data formatting | bytes 4194304
  88.3 0.0 copy-done
  88.3 1.3 %copy.12 = f32[8192,64]{0,1:T(8,128)} copy(f32[8192,64]{0,1:T(8,128)S(1)} %bitcast.8) | data formatting | bytes 4194304
Async XLA Ops:
  85.1 3.2 %copy-start = (f32[64,8192]{1,0:T(8,128)S(1)}, f32[64,8192]{1,0:T(8,128)}, u32[]{:S(2)}) copy-start(f32[64,8192]{1,0:T(8,128)} %get-tuple-element.5) | copy-start | bytes 6291460

commit v2 on v1

v2 whole, which is shorter than its diff:
```python
import jax
import jax.numpy as jnp
from jax import lax
from jax.experimental import pallas as pl
from jax.experimental.pallas import tpu as pltpu
from jax.sharding import Mesh
from jax.sharding import PartitionSpec as P

AXES = ("z", "x", "c", "y")
MESH = pl.DeviceIdType.MESH
F, T, B, R = 128, 64, 2048, 8192
SLAB = 512
NS = B // SLAB
CHUNK = 4096
NCH = R // CHUNK
PIECE = 16
PLANE = 32
LIMIT = 58 << 20
SCALE = 0.5 * 1.4426950408889634
NT = (((1,), (1,)), ((), ()))
NN = (((1,), (0,)), ((), ()))
f32, bf16 = jnp.float32, jnp.bfloat16


def dg(a, b, dims):
    return lax.dot_general(a, b, dims, preferred_element_type=f32)


def rem(a, n):
    return lax.rem(a, jnp.int32(n))


def div(a, n):
    return lax.div(a, jnp.int32(n))


def extra_columns(rows, norm_first):
    wide = rows.astype(f32)
    half_norm = -0.5 * jnp.sum(wide * wide, axis=1, keepdims=True)
    high = half_norm.astype(bf16).astype(f32)
    rest = half_norm - high
    middle = rest.astype(bf16).astype(f32)
    low = rest - middle
    lane = lax.broadcasted_iota(jnp.int32, rows.shape, 1)
    at = 0 if norm_first else 3
    ones_at = 3 - at
    out = jnp.where((lane >= ones_at) & (lane < ones_at + 3), 1.0, 0.0)
    out = jnp.where(lane == at, high, out)
    out = jnp.where(lane == at + 1, middle, out)
    out = jnp.where(lane == at + 2, low, out)
    return out.astype(bf16)


def kernel(
    bid, pts_hbm, tg_hbm, cf_hbm, pr_hbm, inv_hbm, cf, pr,
    km, xa, ca, w16, stage, ihi, ilo, own,
    cand, rbuf, pbuf, zbuf, fbuf,
    part, rs, ysend, ybuf, zsend, zsum, upd, upd16, ubuf, ub,
    lsem, asend, arecv, bsend, brecv, gsend, grecv, usend, urecv,
):
    z, x, c, y = (lax.axis_index(a) for a in AXES)
    me = (x * 4 + y) * 2 + c
    q = x * 2 + c
    block = bid[0]
    quarter = rem(block, 4)
    owner = div(block, 4)
    oy = rem(owner, 4)
    oc = rem(div(owner, 4), 2)
    ox = rem(div(owner, 8), 4)
    oz = div(owner, 32)
    ome = (ox * 4 + oy) * 2 + oc

    def weight(a, b):
        return (a == b).astype(jnp.int32)

    owns = weight(oz, z) * weight(ome, me)

    def pick(index, n, read):
        value = read(0).astype(f32) * weight(index, 0).astype(f32)
        for i in range(1, n):
            value = value + read(i).astype(f32) * weight(index, i).astype(f32)
        return value

    def remote(src, dst, ssem, rsem, dz, dx, dc, dy):
        return pltpu.make_async_remote_copy(
            src_ref=src, dst_ref=dst, send_sem=ssem, recv_sem=rsem,
            device_id=(dz, dx, dc, dy), device_id_type=MESH)

    def plane_peer(d):
        px, py, pc = rem(x + div(d, 8), 4), rem(y + rem(div(d, 2), 4), 4), rem(c + rem(d, 2), 2)
        return (px * 4 + py) * 2 + pc, px, pc, py

    def xc_peer(d):
        peer = rem(q + d, 8)
        return peer, div(peer, 2), rem(peer, 2)

    def loop(low, high, fn):
        lax.fori_loop(low, high, lambda i, t: (fn(i), t)[1], 0)

    def wait_bytes(view, sem):
        pltpu.make_async_copy(view, view, sem).wait()

    points_in = pltpu.make_async_copy(pts_hbm, xa.at[:, pl.ds(0, F)], lsem.at[0])
    points_in.start()
    targets_in = pltpu.make_async_copy(tg_hbm, pr, lsem.at[1])
    targets_in.start()
    coefs_in = pltpu.make_async_copy(cf_hbm, cf, lsem.at[2])
    coefs_in.start()

    def inverse_in(i):
        return pltpu.make_async_copy(inv_hbm.at[pl.ds(i * 128, 128), :], stage.at[i % 2], lsem.at[3 + i % 2])

    inverse_in(0).start()
    inverse_in(1).start()

    barrier = pltpu.get_barrier_semaphore()

    def greet(dz, dx, dc, dy):
        pl.semaphore_signal(barrier, inc=1, device_id=(dz, dx, dc, dy), device_id_type=MESH)

    def greet_plane(d):
        peer, px, pc, py = plane_peer(d)
        greet(z, px, pc, py)

    loop(1, 8, lambda d: greet(rem(z + d, 8), x, c, y))
    loop(1, PLANE, greet_plane)

    def take(k):
        rows = pl.ds(k * SLAB, SLAB)
        cand[rows, :] = pick(quarter, 4, lambda i: xa[pl.ds(i * B + k * SLAB, SLAB), pl.ds(0, F)]).astype(bf16)

    def scatter(k):
        def send(d):
            peer, px, pc, py = plane_peer(d)
            rows = pl.ds(pl.multiple_of(k * SLAB + peer * PIECE, PIECE), PIECE)
            remote(cand.at[rows, :], rbuf.at[k, me], asend.at[k, 0], arecv.at[k, 0], z, px, pc, py).start()

        loop(1, PLANE, send)
        rbuf[k, me] = cand[pl.ds(pl.multiple_of(k * SLAB + me * PIECE, PIECE), PIECE), :]

    def along_z(k):
        wait_bytes(rbuf.at[k, pl.ds(0, PLANE - 1)], arecv.at[k, 0])
        pbuf[k] = pick(ome, PLANE, lambda i: rbuf[k, i]).astype(bf16)
        zbuf[k, z] = pbuf[k]

        def send(d):
            remote(pbuf.at[k], zbuf.at[k, z], asend.at[k, 1], arecv.at[k, 1], rem(z + d, 8), x, c, y).start()

        loop(1, 8, send)

    def gather(k):
        wait_bytes(zbuf.at[k, pl.ds(0, 7)], arecv.at[k, 1])
        fbuf[k] = pick(oz, 8, lambda i: zbuf[k, i]).astype(bf16)
        rows = pl.ds(pl.multiple_of(k * SLAB + me * PIECE, PIECE), PIECE)
        ca[rows, pl.ds(0, F)] = fbuf[k]

        def send(d):
            peer, px, pc, py = plane_peer(d)
            remote(fbuf.at[k], ca.at[rows, pl.ds(0, F)], asend.at[k, 2], arecv.at[k, 2], z, px, pc, py).start()

        loop(1, PLANE, send)

    def finish_centers(k):
        wait_bytes(rbuf.at[k, pl.ds(0, PLANE - 1)], arecv.at[k, 2])
        rows = pl.ds(k * SLAB, SLAB)
        ca[rows, pl.ds(F, F)] = extra_columns(ca[rows, pl.ds(0, F)], True)

    def widen_points(i):
        rows = pl.ds(pl.multiple_of(i * 512, 512), 512)
        xa[rows, pl.ds(F, F)] = extra_columns(xa[rows, pl.ds(0, F)], False)

    def split_inverse(i):
        inverse_in(i).wait()
        rows = pl.ds(i * 128, 128)
        value = stage[i % 2]
        high = value.astype(bf16)
        ihi[rows, :] = high
        ilo[rows, :] = (value - high.astype(f32)).astype(bf16)
        if i + 2 < SLAB // 128:
            inverse_in(i + 2).start()

    def narrow(i):
        cols = pl.ds(pl.multiple_of(i * 1024, 1024), 1024)
        w16[:, cols] = cf[:, cols].astype(bf16)

    points_in.wait()
    take(0)
    pl.semaphore_wait(barrier, PLANE - 1 + 7)
    scatter(0)
    take(1)
    loop(0, R // 1024, widen_points)
    scatter(1)
    take(2)
    take(3)
    along_z(0)
    scatter(2)
    loop(R // 1024, R // 512, widen_points)
    along_z(1)
    scatter(3)
    coefs_in.wait()
    targets_in.wait()
    loop(0, R // 1024, narrow)
    own[...] = pick(quarter, 4, lambda k: pr[:, pl.ds(k * B, B)] - cf[:, pl.ds(k * B, B)]) * owns.astype(f32)
    preds_in = pltpu.make_async_copy(pr_hbm, pr, lsem.at[1])
    preds_in.start()
    gather(0)
    along_z(2)
    split_inverse(0)
    split_inverse(1)
    gather(1)
    along_z(3)
    split_inverse(2)
    split_inverse(3)
    finish_centers(0)

    def slab_work(s):
        cols = pl.ds(s * SLAB, SLAB)
        part[s] = own[:, cols]

        def step(j):
            rows = pl.ds(pl.multiple_of(j * CHUNK, CHUNK), CHUNK)
            exponent = dg(xa[rows, :], ca[cols, :], NT)
            tile = jnp.exp2(exponent * SCALE).astype(bf16)
            km[rows, cols] = tile
            part[s] -= dg(w16[:, rows], tile, NN)

        loop(0, NCH, step)

        def send(d):
            peer, px, pc = xc_peer(d)
            rows = pl.ds(pl.multiple_of(peer * 8, 8), 8)
            remote(part.at[s, rows, :], rs.at[s, q], bsend.at[s, 0], brecv.at[s, 0], z, px, pc, y).start()

        loop(1, 8, send)
        rs[s, q] = part[s, pl.ds(pl.multiple_of(q * 8, 8), 8), :]

    def total(ref, s, n):
        value = ref[s, 0]
        for i in range(1, n):
            value = value + ref[s, i]
        return value

    def over_y(s):
        wait_bytes(rs.at[s, pl.ds(0, 7)], brecv.at[s, 0])
        value = total(rs, s, 8)
        ysend[s] = value
        ybuf[s, y] = value

        def send(d):
            remote(ysend.at[s], ybuf.at[s, y], bsend.at[s, 1], brecv.at[s, 1], z, x, c, rem(y + d, 4)).start()

        loop(1, 4, send)

    def over_z(s):
        wait_bytes(ybuf.at[s, pl.ds(0, 3)], brecv.at[s, 1])
        value = total(ybuf, s, 4)
        zsend[s] = value
        zsum[s, z] = value

        def send(d):
            remote(zsend.at[s], zsum.at[s, z], bsend.at[s, 2], brecv.at[s, 2], rem(z + d, 8), x, c, y).start()

        loop(1, 8, send)

    def apply_inverse(s):
        wait_bytes(zsum.at[s, pl.ds(0, 7)], brecv.at[s, 2])
        residual = total(zsum, s, 8)
        high = residual.astype(bf16).astype(f32)
        both = jnp.concatenate([high, residual - high], axis=0).astype(bf16)
        cols = pl.ds(s * SLAB, SLAB)
        by_high = dg(both, ihi[:, cols], NT)
        by_low = dg(both, ilo[:, cols], NT)
        add = by_high[0:8] + by_high[8:16] + by_low[0:8]
        upd[...] = add if s == 0 else upd[...] + add

    for t in range(NS + 3):
        if t < NS:
            slab_work(t)
        if t == 0:
            gather(2)
            gather(3)
        if t + 1 < NS:
            finish_centers(t + 1)
        if 0 <= t - 1 < NS:
            over_y(t - 1)
        if 0 <= t - 2 < NS:
            over_z(t - 2)
        if 0 <= t - 3 < NS:
            apply_inverse(t - 3)

    upd16[...] = upd[...].astype(bf16)
    ubuf[q] = upd16[...]

    def gather_update(d):
        peer, px, pc = xc_peer(d)
        remote(upd16, ubuf.at[q], gsend.at[0], grecv.at[0], z, px, pc, y).start()

    loop(1, 8, gather_update)
    wait_bytes(ubuf.at[pl.ds(0, 7)], grecv.at[0])
    ub[y] = jnp.concatenate([ubuf[i].astype(f32) for i in range(8)], axis=0).astype(bf16)

    def share_update(d):
        remote(ub.at[y], ub.at[y], usend.at[0], urecv.at[0], z, x, c, rem(y + d, 4)).start()

    loop(1, 4, share_update)
    preds_in.wait()

    def product(rows, slabs):
        total = None
        for slab in slabs:
            cols = pl.ds(pl.multiple_of(slab * SLAB, SLAB), SLAB)
            one = dg(km[rows, cols], ub[slab], NT)
            total = one if total is None else total + one
        return total.T

    def advance_own(j):
        rows = pl.ds(pl.multiple_of(j * CHUNK, CHUNK), CHUNK)
        pr[:, rows] += product(rows, (y,))

    loop(0, NCH, advance_own)
    wait_bytes(ub.at[pl.ds(0, 3)], urecv.at[0])
    for s in range(NS):
        for k in range(4):
            cols = pl.ds(k * B + s * SLAB, SLAB)
            cf[:, cols] += ub[s].astype(f32) * (owns * weight(quarter, k)).astype(f32)

    def advance(j):
        rows = pl.ds(pl.multiple_of(j * 2048, 2048), 2048)
        pr[:, rows] += product(rows, tuple(rem(y + d, 4) for d in (1, 2, 3)))

    loop(0, R // 2048, advance)

    for k in range(NS):
        wait_bytes(rbuf.at[k, pl.ds(0, PLANE - 1)], asend.at[k, 0])
        wait_bytes(zbuf.at[k, pl.ds(0, 7)], asend.at[k, 1])
        wait_bytes(rbuf.at[k, pl.ds(0, PLANE - 1)], asend.at[k, 2])
    for s in range(NS):
        wait_bytes(rs.at[s, pl.ds(0, 7)], bsend.at[s, 0])
        wait_bytes(ybuf.at[s, pl.ds(0, 3)], bsend.at[s, 1])
        wait_bytes(zsum.at[s, pl.ds(0, 7)], bsend.at[s, 2])
    wait_bytes(ubuf.at[pl.ds(0, 7)], gsend.at[0])
    wait_bytes(ub.at[pl.ds(0, 3)], usend.at[0])


def write_out(cf, pr, nc_hbm, np_hbm, sem):
    copies = [pltpu.make_async_copy(cf, nc_hbm, sem.at[0]), pltpu.make_async_copy(pr, np_hbm, sem.at[1])]
    for copy in copies:
        copy.start()
    for copy in copies:
        copy.wait()


def body(points, targets, coefs, preds, block_inverse, block_id):
    hbm = pl.BlockSpec(memory_space=pl.ANY)
    vmem = pl.BlockSpec(memory_space=pltpu.VMEM)
    V, D = pltpu.VMEM, pltpu.SemaphoreType.DMA
    new_coefs, new_preds = pl.pallas_call(
        kernel,
        name="ridge_step",
        in_specs=[pl.BlockSpec(memory_space=pltpu.SMEM)] + [hbm] * 5,
        out_specs=[vmem, vmem],
        out_shape=[V((T, R), f32)] * 2,
        scratch_shapes=[
            V((R, B), bf16), V((R, 2 * F), bf16), V((B, 2 * F), bf16), V((T, R), bf16),
            V((2, 128, B), f32), V((SLAB, B), bf16), V((SLAB, B), bf16), V((T, B), f32),
            V((B, F), bf16), V((NS, PLANE, PIECE, F), bf16), V((NS, PIECE, F), bf16), V((NS, 8, PIECE, F), bf16), V((NS, PIECE, F), bf16),
            V((NS, T, SLAB), f32), V((NS, 8, 8, SLAB), f32), V((NS, 8, SLAB), f32), V((NS, 4, 8, SLAB), f32),
            V((NS, 8, SLAB), f32), V((NS, 8, 8, SLAB), f32), V((8, SLAB), f32), V((8, SLAB), bf16), V((8, 8, SLAB), bf16), V((4, T, SLAB), bf16),
            D((5,)), D((NS, 3)), D((NS, 3)), D((NS, 3)), D((NS, 3)), D((1,)), D((1,)), D((1,)), D((1,)),
        ],
        compiler_params=pltpu.CompilerParams(collective_id=0, has_side_effects=True, vmem_limit_bytes=LIMIT),
    )(block_id, points, targets.T, coefs.T, preds.T, block_inverse)
    new_coefs, new_preds = pl.pallas_call(
        write_out,
        name="write_out",
        in_specs=[vmem, vmem],
        out_specs=[hbm, hbm],
        out_shape=[jax.ShapeDtypeStruct((T, R), f32)] * 2,
        scratch_shapes=[D((2,))],
        compiler_params=pltpu.CompilerParams(has_side_effects=True, vmem_limit_bytes=1 << 20),
    )(new_coefs, new_preds)
    return new_coefs.T, new_preds.T


def solution(mesh):
    split = Mesh(mesh.devices.reshape(8, 4, 2, mesh.shape["blk"]), AXES)
    rows = P(AXES, None)
    return jax.shard_map(
        body, mesh=split, in_specs=(rows, rows, rows, rows, P("y", None), P()), out_specs=(rows, rows), check_vma=False)
```

time: 89.9 us -> 80.6 us (0.90)
  Pallas kernels: 83.8 us -> 79.2 us
  local copies, waits for them, and re-layouts: 4.53 us -> 0 us
    pallas_call x1, Pallas kernels: 83.8 us -> 77.2 us  [body(): pl.pallas_call(kernel, name='ridge_step', in_specs=[pl.BlockSpec(memory_s...]
    unnamed x4 -> x0, local copies, waits for them, and re-layouts: 4.53 us -> none
    pallas_call x0 -> x1, Pallas kernels: none -> 2.03 us  [body(): pl.pallas_call(write_out, name='write_out', in_specs=[vmem, vmem], out_sp...]
where the time goes in v2:
time: 80.6 us; the launch traced here: 80.5 us
  Pallas kernels  79.2 us (98%)
  between operations  1.29 us (2%)
    pallas_call x1, Pallas kernels, body(): pl.pallas_call(kernel, name='ridge_step', in_specs=[pl.BlockSpec(memory_s...  77.2 us
    pallas_call x1, Pallas kernels, body(): pl.pallas_call(write_out, name='write_out', in_specs=[vmem, vmem], out_sp...  2.03 us

profile of v2, /device:TPU:1, one launch (start us, length us, event | category | flops | bytes accessed | tf_op | source)
XLA Modules:
  0.0 80.5 jit_solution(1750656024345466728)
XLA Ops:
  1.3 77.2 %ridge_step.1 = (f32[64,8192]{1,0:T(8,128)S(1)}, f32[64,8192]{1,0:T(8,128)S(1)}) custom-call(s32[1]{0:T(128)S(6)} %copy.8.bid, bf16[8192,128]{1,0:T(8,128)(2,1)} %pts_hbm.1, f32[64,8192]{1,0:T(8,128)} %bitcast.5, f32[64,8192]{1,0:T(8,128)} %bitcast.6, f32[64,8192]{1,0:T(8,128)} %bitcast.7, f32[512,2048]{1,0:T(8,128)} %inv_hbm.1), custom_call_target="tpu_custom_call" | custom-call | tf_op jit(solution)/shard_map/ridge_step/pallas_call | solution.py:357
  78.5 2.0 %write_out.1 = (f32[64,8192]{1,0:T(8,128)}, f32[64,8192]{1,0:T(8,128)}) custom-call(f32[64,8192]{1,0:T(8,128)S(1)} %get-tuple-element.6.cf, f32[64,8192]{1,0:T(8,128)S(1)} %get-tuple-element.7.pr), custom_call_target="tpu_custom_call" | custom-call | tf_op jit(solution)/shard_map/write_out/pallas_call | solution.py:373

commit v3 on v2

v3 whole, which is shorter than its diff:
```python
import jax
import jax.numpy as jnp
from jax import lax
from jax.experimental import pallas as pl
from jax.experimental.pallas import tpu as pltpu
from jax.sharding import Mesh
from jax.sharding import PartitionSpec as P

AXES = ("z", "x", "c", "y")
MESH = pl.DeviceIdType.MESH
F, T, B, R = 128, 64, 2048, 8192
SLAB = 512
NS = B // SLAB
CHUNK = 4096
PIECE = 16
PLANE = 16
HALF = SLAB // 2
LIMIT = 50 << 20
FIRST = 6144
STEP = 3072
SCALE = 0.5 * 1.4426950408889634
NT = (((1,), (1,)), ((), ()))
NN = (((1,), (0,)), ((), ()))
f32, bf16 = jnp.float32, jnp.bfloat16


def dg(a, b, dims):
    return lax.dot_general(a, b, dims, preferred_element_type=f32)


def rem(a, n):
    return lax.rem(a, jnp.int32(n))


def div(a, n):
    return lax.div(a, jnp.int32(n))


def extra_columns(rows, norm_first):
    wide = rows.astype(f32)
    half_norm = -0.5 * jnp.sum(wide * wide, axis=1, keepdims=True)
    high = half_norm.astype(bf16).astype(f32)
    rest = half_norm - high
    middle = rest.astype(bf16).astype(f32)
    low = rest - middle
    lane = lax.broadcasted_iota(jnp.int32, rows.shape, 1)
    at = 0 if norm_first else 3
    ones_at = 3 - at
    out = jnp.where((lane >= ones_at) & (lane < ones_at + 3), 1.0, 0.0)
    out = jnp.where(lane == at, high, out)
    out = jnp.where(lane == at + 1, middle, out)
    out = jnp.where(lane == at + 2, low, out)
    return out.astype(bf16)


def slab_cols(s):
    return pl.ds(s * SLAB, SLAB) if isinstance(s, int) else pl.ds(pl.multiple_of(s * SLAB, SLAB), SLAB)


def product(km, ub, rows, slabs):
    total = None
    for slab in slabs:
        one = dg(km[rows, slab_cols(slab)], ub[slab], NT)
        total = one if total is None else total + one
    return total.T


def kernel(
    bid, pts_hbm, tg_hbm, cf_hbm, pr_hbm, inv_hbm, cf, pr, kept, u_out,
    km, xa, ca, w16, stage, ihi, ilo, own,
    cand, crecv, hb, rbuf, pbuf, zbuf, fbuf,
    part, rs, ysend, ybuf, zsend, zsum, upd, upd16, ubuf, ub,
    lsem, asend, arecv, bsend, brecv, gsend, grecv, usend, urecv,
):
    z, x, c, y = (lax.axis_index(a) for a in AXES)
    plane = x * 4 + y
    q = x * 2 + c
    block = bid[0]
    quarter = rem(block, 4)
    owner = div(block, 4)
    oy = rem(owner, 4)
    oc = rem(div(owner, 4), 2)
    ox = rem(div(owner, 8), 4)
    oz = div(owner, 32)
    oplane = ox * 4 + oy

    def weight(a, b):
        return (a == b).astype(jnp.int32)

    owns = weight(oz, z) * weight(oplane, plane) * weight(oc, c)

    def pick(index, n, read):
        value = read(0).astype(f32) * weight(index, 0).astype(f32)
        for i in range(1, n):
            value = value + read(i).astype(f32) * weight(index, i).astype(f32)
        return value

    def remote(src, dst, ssem, rsem, dz, dx, dc, dy):
        return pltpu.make_async_remote_copy(
            src_ref=src, dst_ref=dst, send_sem=ssem, recv_sem=rsem,
            device_id=(dz, dx, dc, dy), device_id_type=MESH)

    def plane_peer(d):
        return rem(x + div(d, 8), 4), rem(c + rem(d, 2), 2), rem(y + rem(div(d, 2), 4), 4)

    def z_peer(i):
        half = div(i, 2)
        return rem(z + 4 + half - rem(i, 2) * (half + div(i + 1, 2)), 8)

    def xc_peers():
        for dx, dc in ((2, 0), (2, 1), (1, 0), (3, 0), (1, 1), (3, 1), (0, 1)):
            px, pc = rem(x + dx, 4), rem(c + dc, 2)
            yield px * 2 + pc, px, pc

    def loop(low, high, fn):
        lax.fori_loop(low, high, lambda i, t: (fn(i), t)[1], 0)

    def wait_bytes(view, sem):
        pltpu.make_async_copy(view, view, sem).wait()

    points_in = pltpu.make_async_copy(pts_hbm, xa.at[:, pl.ds(0, F)], lsem.at[0])
    points_in.start()
    targets_in = pltpu.make_async_copy(tg_hbm, pr, lsem.at[1])
    targets_in.start()
    coefs_in = pltpu.make_async_copy(cf_hbm, cf, lsem.at[2])
    coefs_in.start()

    def inverse_in(i):
        return pltpu.make_async_copy(inv_hbm.at[pl.ds(i * 128, 128), :], stage.at[i % 2], lsem.at[3 + i % 2])

    inverse_in(0).start()
    inverse_in(1).start()

    barrier = pltpu.get_barrier_semaphore()

    def greet(dz, dx, dc, dy):
        pl.semaphore_signal(barrier, inc=1, device_id=(dz, dx, dc, dy), device_id_type=MESH)

    def greet_plane(d):
        greet(z, *plane_peer(d))

    loop(1, 8, lambda d: greet(rem(z + d, 8), x, c, y))
    loop(1, 2 * PLANE, greet_plane)

    my_rows = [pl.ds(pl.multiple_of(k * SLAB + c * HALF + plane * PIECE, PIECE), PIECE) for k in range(NS)]

    def take(k):
        rows = pl.ds(k * SLAB, SLAB)
        cand[rows, :] = pick(quarter, 4, lambda i: xa[pl.ds(i * B + k * SLAB, SLAB), pl.ds(0, F)]).astype(bf16)

    def swap(k):
        rows = pl.ds(pl.multiple_of(k * SLAB + (1 - c) * HALF, HALF), HALF)
        remote(cand.at[rows, :], crecv.at[k], asend.at[k, 3], arecv.at[k, 3], z, x, 1 - c, y).start()

    def scatter(k):
        wait_bytes(crecv.at[k], arecv.at[k, 3])
        own_half = cand[pl.ds(pl.multiple_of(k * SLAB + c * HALF, HALF), HALF), :]
        hb[k] = pick(weight(oc, c), 2, lambda i: own_half if i else crecv[k]).astype(bf16)

        def send(d):
            px, py = rem(x + div(d, 4), 4), rem(y + rem(d, 4), 4)
            rows = pl.ds(pl.multiple_of((px * 4 + py) * PIECE, PIECE), PIECE)
            remote(hb.at[k, rows, :], rbuf.at[k, plane], asend.at[k, 0], arecv.at[k, 0], z, px, c, py).start()

        loop(1, PLANE, send)
        rbuf[k, plane] = hb[k, pl.ds(pl.multiple_of(plane * PIECE, PIECE), PIECE), :]

    def along_z(k):
        wait_bytes(rbuf.at[k, pl.ds(0, PLANE - 1)], arecv.at[k, 0])
        pbuf[k] = pick(oplane, PLANE, lambda i: rbuf[k, i]).astype(bf16)
        zbuf[k, z] = pbuf[k]

        def send(d):
            remote(pbuf.at[k], zbuf.at[k, z], asend.at[k, 1], arecv.at[k, 1], z_peer(d), x, c, y).start()

        loop(0, 7, send)

    def gather(k):
        wait_bytes(zbuf.at[k, pl.ds(0, 7)], arecv.at[k, 1])
        fbuf[k] = pick(oz, 8, lambda i: zbuf[k, i]).astype(bf16)
        ca[my_rows[k], pl.ds(0, F)] = fbuf[k]

        def send(d):
            remote(fbuf.at[k], ca.at[my_rows[k], pl.ds(0, F)], asend.at[k, 2], arecv.at[k, 2], z, *plane_peer(d)).start()

        loop(1, 2 * PLANE, send)

    gathered = ca.at[pl.ds(0, (2 * PLANE - 1) * PIECE), pl.ds(0, F)]

    def finish_centers(k):
        wait_bytes(gathered, arecv.at[k, 2])
        rows = slab_cols(k)
        ca[rows, pl.ds(F, F)] = extra_columns(ca[rows, pl.ds(0, F)], True)

    def widen_points(i):
        rows = pl.ds(pl.multiple_of(i * 512, 512), 512)
        xa[rows, pl.ds(F, F)] = extra_columns(xa[rows, pl.ds(0, F)], False)

    def split_inverse(i):
        inverse_in(i).wait()
        rows = pl.ds(i * 128, 128)
        value = stage[i % 2]
        high = value.astype(bf16)
        ihi[rows, :] = high
        ilo[rows, :] = (value - high.astype(f32)).astype(bf16)
        if i + 2 < SLAB // 128:
            inverse_in(i + 2).start()

    def narrow(i):
        cols = pl.ds(pl.multiple_of(i * 1024, 1024), 1024)
        w16[:, cols] = cf[:, cols].astype(bf16)

    points_in.wait()
    for k in range(NS):
        take(k)
    pl.semaphore_wait(barrier, 2 * PLANE - 1 + 7)
    for k in range(NS):
        swap(k)
    scatter(0)
    loop(0, R // 1024, widen_points)
    scatter(1)
    loop(R // 1024, R // 512, widen_points)
    along_z(0)
    scatter(2)
    along_z(1)
    scatter(3)
    coefs_in.wait()
    targets_in.wait()
    loop(0, R // 1024, narrow)
    own[...] = pick(quarter, 4, lambda k: pr[:, pl.ds(k * B, B)] - cf[:, pl.ds(k * B, B)]) * owns.astype(f32)
    preds_in = pltpu.make_async_copy(pr_hbm, pr, lsem.at[1])
    preds_in.start()
    gather(0)
    along_z(2)
    split_inverse(0)
    split_inverse(1)
    gather(1)
    along_z(3)
    split_inverse(2)
    split_inverse(3)
    gather(2)
    finish_centers(0)

    def slab_work(s):
        cols = slab_cols(s)
        part[s] = own[:, cols]

        for low in range(0, R, CHUNK):
            rows = pl.ds(low, CHUNK)
            exponent = dg(xa[rows, :], ca[cols, :], NT)
            tile = jnp.exp2(exponent * SCALE).astype(bf16)
            if low + CHUNK <= FIRST:
                km[rows, cols] = tile
            else:
                km[pl.ds(low, FIRST - low), cols] = tile[: FIRST - low]
                kept[:, cols] = tile[FIRST - low :]
            part[s] -= dg(w16[:, rows], tile, NN)

        for peer, px, pc in xc_peers():
            rows = pl.ds(pl.multiple_of(peer * 8, 8), 8)
            remote(part.at[s, rows, :], rs.at[s, q], bsend.at[s, 0], brecv.at[s, 0], z, px, pc, y).start()
        rs[s, q] = part[s, pl.ds(pl.multiple_of(q * 8, 8), 8), :]

    def total(ref, s, n):
        value = ref[s, 0]
        for i in range(1, n):
            value = value + ref[s, i]
        return value

    def over_y(s):
        wait_bytes(rs.at[s, pl.ds(0, 7)], brecv.at[s, 0])
        value = total(rs, s, 8)
        ysend[s] = value
        ybuf[s, y] = value

        for d in (2, 1, 3):
            remote(ysend.at[s], ybuf.at[s, y], bsend.at[s, 1], brecv.at[s, 1], z, x, c, rem(y + d, 4)).start()

    def over_z(s):
        wait_bytes(ybuf.at[s, pl.ds(0, 3)], brecv.at[s, 1])
        value = total(ybuf, s, 4)
        zsend[s] = value
        zsum[s, z] = value

        def send(d):
            remote(zsend.at[s], zsum.at[s, z], bsend.at[s, 2], brecv.at[s, 2], z_peer(d), x, c, y).start()

        loop(0, 7, send)

    def apply_inverse(s):
        wait_bytes(zsum.at[s, pl.ds(0, 7)], brecv.at[s, 2])
        residual = total(zsum, s, 8)
        high = residual.astype(bf16).astype(f32)
        both = jnp.concatenate([high, residual - high], axis=0).astype(bf16)
        cols = slab_cols(s)
        by_high = dg(both, ihi[:, cols], NT)
        by_low = dg(both, ilo[:, cols], NT)
        upd[...] += by_high[0:8] + by_high[8:16] + by_low[0:8]

    upd[...] = jnp.zeros_like(upd)

    def slab_step(t):
        slab_work(t)
        pl.when(t == 0)(lambda: gather(NS - 1))
        pl.when(t < NS - 1)(lambda: finish_centers(t + 1))
        pl.when(t >= 1)(lambda: over_y(t - 1))
        pl.when(t >= 2)(lambda: over_z(t - 2))

    loop(0, NS, slab_step)
    apply_inverse(0)
    over_y(NS - 1)
    over_z(NS - 2)
    apply_inverse(1)
    over_z(NS - 1)
    apply_inverse(2)
    apply_inverse(3)

    upd16[...] = upd[...].astype(bf16)
    ubuf[q] = upd16[...]

    for peer, px, pc in xc_peers():
        remote(upd16, ubuf.at[q], gsend.at[0], grecv.at[0], z, px, pc, y).start()
    wait_bytes(ubuf.at[pl.ds(0, 7)], grecv.at[0])
    ub[y] = jnp.concatenate([ubuf[i].astype(f32) for i in range(8)], axis=0).astype(bf16)

    def share_update(d):
        kind = d % 2
        remote(ub.at[y], ub.at[y], usend.at[kind], urecv.at[kind], z, x, c, rem(y + d, 4)).start()

    share_update(1)
    share_update(3)
    preds_in.wait()

    def advance(*slabs):
        def step(j):
            rows = pl.ds(pl.multiple_of(j * STEP, STEP), STEP)
            pr[:, rows] += product(km, ub, rows, slabs)

        loop(0, FIRST // STEP, step)

    advance(y)
    share_update(2)
    wait_bytes(ub.at[pl.ds(0, 2)], urecv.at[1])
    advance(rem(y + 1, 4), rem(y + 3, 4))
    wait_bytes(ub.at[0], urecv.at[0])
    for s in range(NS):
        u_out[:, slab_cols(s)] = ub[s]
        for k in range(4):
            cols = pl.ds(k * B + s * SLAB, SLAB)
            cf[:, cols] += ub[s].astype(f32) * (owns * weight(quarter, k)).astype(f32)
    advance(rem(y + 2, 4))

    for k in range(NS):
        wait_bytes(rbuf.at[k, pl.ds(0, PLANE - 1)], asend.at[k, 0])
        wait_bytes(zbuf.at[k, pl.ds(0, 7)], asend.at[k, 1])
        wait_bytes(gathered, asend.at[k, 2])
        wait_bytes(crecv.at[k], asend.at[k, 3])
    for s in range(NS):
        wait_bytes(rs.at[s, pl.ds(0, 7)], bsend.at[s, 0])
        wait_bytes(ybuf.at[s, pl.ds(0, 3)], bsend.at[s, 1])
        wait_bytes(zsum.at[s, pl.ds(0, 7)], bsend.at[s, 2])
    wait_bytes(ubuf.at[pl.ds(0, 7)], gsend.at[0])
    wait_bytes(ub.at[0], usend.at[0])
    wait_bytes(ub.at[pl.ds(0, 2)], usend.at[1])


def finish(cf, pr, kept, u, nc_hbm, np_hbm, out, sem):
    done, rest = pl.ds(0, FIRST), pl.ds(FIRST, R - FIRST)
    copies = [pltpu.make_async_copy(cf, nc_hbm, sem.at[0]), pltpu.make_async_copy(pr.at[:, done], np_hbm.at[:, done], sem.at[1])]
    for copy in copies:
        copy.start()
    out[...] = pr[:, rest] + dg(kept[...], u[...], NT).T
    copies.append(pltpu.make_async_copy(out, np_hbm.at[:, rest], sem.at[2]))
    copies[-1].start()
    for copy in copies:
        copy.wait()


def body(points, targets, coefs, preds, block_inverse, block_id):
    hbm = pl.BlockSpec(memory_space=pl.ANY)
    vmem = pl.BlockSpec(memory_space=pltpu.VMEM)
    V, D = pltpu.VMEM, pltpu.SemaphoreType.DMA
    kept = pl.pallas_call(
        kernel,
        name="ridge_step",
        in_specs=[pl.BlockSpec(memory_space=pltpu.SMEM)] + [hbm] * 5,
        out_specs=[vmem] * 4,
        out_shape=[V((T, R), f32), V((T, R), f32), V((R - FIRST, B), bf16), V((T, B), bf16)],
        scratch_shapes=[
            V((FIRST, B), bf16), V((R, 2 * F), bf16), V((B, 2 * F), bf16), V((T, R), bf16),
            V((2, 128, B), f32), V((SLAB, B), bf16), V((SLAB, B), bf16), V((T, B), f32),
            V((B, F), bf16), V((NS, HALF, F), bf16), V((NS, HALF, F), bf16), V((NS, PLANE, PIECE, F), bf16), V((NS, PIECE, F), bf16), V((NS, 8, PIECE, F), bf16), V((NS, PIECE, F), bf16),
            V((NS, T, SLAB), f32), V((NS, 8, 8, SLAB), f32), V((NS, 8, SLAB), f32), V((NS, 4, 8, SLAB), f32),
            V((NS, 8, SLAB), f32), V((NS, 8, 8, SLAB), f32), V((8, SLAB), f32), V((8, SLAB), bf16), V((8, 8, SLAB), bf16), V((4, T, SLAB), bf16),
            D((5,)), D((NS, 4)), D((NS, 4)), D((NS, 3)), D((NS, 3)), D((1,)), D((1,)), D((2,)), D((2,)),
        ],
        compiler_params=pltpu.CompilerParams(collective_id=0, has_side_effects=True, vmem_limit_bytes=LIMIT),
    )(block_id, points, targets.T, coefs.T, preds.T, block_inverse)
    new_coefs, new_preds = pl.pallas_call(
        finish,
        name="finish",
        in_specs=[vmem] * 4,
        out_specs=[hbm, hbm],
        out_shape=[jax.ShapeDtypeStruct((T, R), f32)] * 2,
        scratch_shapes=[V((T, R - FIRST), f32), D((3,))],
        compiler_params=pltpu.CompilerParams(has_side_effects=True, vmem_limit_bytes=12 << 20),
    )(*kept)
    return new_coefs.T, new_preds.T


def solution(mesh):
    split = Mesh(mesh.devices.reshape(8, 4, 2, mesh.shape["blk"]), AXES)
    rows = P(AXES, None)
    return jax.shard_map(
        body, mesh=split, in_specs=(rows, rows, rows, rows, P("y", None), P()), out_specs=(rows, rows), check_vma=False)
```

time: 80.6 us -> 76.1 us (0.944)
  Pallas kernels: 79.2 us -> 74.7 us
    pallas_call x1, Pallas kernels: 77.2 us -> 71.2 us  [body(): pl.pallas_call(kernel, name='ridge_step', in_specs=[pl.BlockSpec(memory_s...]
    pallas_call x1, Pallas kernels: 2.03 us -> 3.49 us  [body(): pl.pallas_call(finish, name='finish', in_specs=[vmem] * 4, out_specs=[hbm...]
where the time goes in v3:
time: 76.1 us; the launch traced here: 76 us
  Pallas kernels  74.7 us (98%)
  between operations  1.29 us (2%)
    pallas_call x1, Pallas kernels, body(): pl.pallas_call(kernel, name='ridge_step', in_specs=[pl.BlockSpec(memory_s...  71.2 us
    pallas_call x1, Pallas kernels, body(): pl.pallas_call(finish, name='finish', in_specs=[vmem] * 4, out_specs=[hbm...  3.49 us

profile of v3, /device:TPU:1, one launch (start us, length us, event | category | flops | bytes accessed | tf_op | source)
XLA Modules:
  0.0 76.0 jit_solution(17267612972795076133)
XLA Ops:
  1.3 71.2 %ridge_step.1 = (f32[64,8192]{1,0:T(8,128)S(1)}, f32[64,8192]{1,0:T(8,128)S(1)}, bf16[2048,2048]{1,0:T(8,128)(2,1)S(1)}, bf16[64,2048]{1,0:T(8,128)(2,1)S(1)}) custom-call(s32[1]{0:T(128)S(6)} %copy.8.bid, bf16[8192,128]{1,0:T(8,128)(2,1)} %pts_hbm.1, f32[64,8192]{1,0:T(8,128)} %bitcast.5, f32[64,8192]{1,0:T(8,128)} %bitcast.6, f32[64,8192]{1,0:T(8,128)} %bitcast.7, ...), custom_call_target="tpu_custom_call" | custom-call | tf_op jit(solution)/shard_map/ridge_step/pallas_call | solution.py:383
  72.5 3.5 %finish.1 = (f32[64,8192]{1,0:T(8,128)}, f32[64,8192]{1,0:T(8,128)}) custom-call(f32[64,8192]{1,0:T(8,128)S(1)} %get-tuple-element.8.cf, f32[64,8192]{1,0:T(8,128)S(1)} %get-tuple-element.9.pr, bf16[2048,2048]{1,0:T(8,128)(2,1)S(1)} %get-tuple-element.10.kept, bf16[64,2048]{1,0:T(8,128)(2,1)S(1)} %get-tuple-element.11.u), custom_call_target="tpu_custom_call" | custom-call | tf_op jit(solution)/shard_map/finish/pallas_call | solution.py:399

commit v4 on v3

--- a/solution.py
+++ b/solution.py
@@ -100,8 +100,16 @@
             src_ref=src, dst_ref=dst, send_sem=ssem, recv_sem=rsem,
             device_id=(dz, dx, dc, dy), device_id_type=MESH)
 
-    def plane_peer(d):
-        return rem(x + div(d, 8), 4), rem(c + rem(d, 2), 2), rem(y + rem(div(d, 2), 4), 4)
+    def to_plane(start):
+        for dx in (2, 1, 3, 0):
+            px = rem(x + dx, 4)
+
+            def near(i, px=px):
+                start(px, rem(c + 1 + rem(i, 2), 2), rem(y + 2 + div(i, 2), 4))
+
+            loop(0, 8 if dx else 5, near)
+        start(x, 1 - c, rem(y + 1, 4))
+        start(x, c, rem(y + 1, 4))
 
     def z_peer(i):
         half = div(i, 2)
@@ -136,11 +144,8 @@
     def greet(dz, dx, dc, dy):
         pl.semaphore_signal(barrier, inc=1, device_id=(dz, dx, dc, dy), device_id_type=MESH)
 
-    def greet_plane(d):
-        greet(z, *plane_peer(d))
-
-    loop(1, 8, lambda d: greet(rem(z + d, 8), x, c, y))
-    loop(1, 2 * PLANE, greet_plane)
+    loop(0, 7, lambda i: greet(z_peer(i), x, c, y))
+    to_plane(lambda px, pc, py: greet(z, px, pc, py))
 
     my_rows = [pl.ds(pl.multiple_of(k * SLAB + c * HALF + plane * PIECE, PIECE), PIECE) for k in range(NS)]
 
@@ -157,12 +162,13 @@
         own_half = cand[pl.ds(pl.multiple_of(k * SLAB + c * HALF, HALF), HALF), :]
         hb[k] = pick(weight(oc, c), 2, lambda i: own_half if i else crecv[k]).astype(bf16)
 
-        def send(d):
-            px, py = rem(x + div(d, 4), 4), rem(y + rem(d, 4), 4)
+        def send(px, py):
             rows = pl.ds(pl.multiple_of((px * 4 + py) * PIECE, PIECE), PIECE)
             remote(hb.at[k, rows, :], rbuf.at[k, plane], asend.at[k, 0], arecv.at[k, 0], z, px, c, py).start()
 
-        loop(1, PLANE, send)
+        for dx in (2, 1, 3, 0):
+            px = rem(x + dx, 4)
+            loop(0 if dx else 1, 4, lambda i, px=px, dx=dx: send(px, rem(y + 2 + i, 4) if dx else rem(y + i, 4)))
         rbuf[k, plane] = hb[k, pl.ds(pl.multiple_of(plane * PIECE, PIECE), PIECE), :]
 
     def along_z(k):
@@ -180,10 +186,8 @@
         fbuf[k] = pick(oz, 8, lambda i: zbuf[k, i]).astype(bf16)
         ca[my_rows[k], pl.ds(0, F)] = fbuf[k]
 
-        def send(d):
-            remote(fbuf.at[k], ca.at[my_rows[k], pl.ds(0, F)], asend.at[k, 2], arecv.at[k, 2], z, *plane_peer(d)).start()
-
-        loop(1, 2 * PLANE, send)
+        to_plane(lambda px, pc, py: remote(
+            fbuf.at[k], ca.at[my_rows[k], pl.ds(0, F)], asend.at[k, 2], arecv.at[k, 2], z, px, pc, py).start())
 
     gathered = ca.at[pl.ds(0, (2 * PLANE - 1) * PIECE), pl.ds(0, F)]
 
@@ -340,14 +344,16 @@
 
     advance(y)
     share_update(2)
+    rest = pl.ds(FIRST, R - FIRST)
+    pr[:, rest] += dg(kept[:, slab_cols(y)], ub[y], NT).T
     wait_bytes(ub.at[pl.ds(0, 2)], urecv.at[1])
     advance(rem(y + 1, 4), rem(y + 3, 4))
     wait_bytes(ub.at[0], urecv.at[0])
     for s in range(NS):
-        u_out[:, slab_cols(s)] = ub[s]
         for k in range(4):
             cols = pl.ds(k * B + s * SLAB, SLAB)
             cf[:, cols] += ub[s].astype(f32) * (owns * weight(quarter, k)).astype(f32)
+    u_out[...] = ub[...]
     advance(rem(y + 2, 4))
 
     for k in range(NS):
@@ -369,7 +375,8 @@
     copies = [pltpu.make_async_copy(cf, nc_hbm, sem.at[0]), pltpu.make_async_copy(pr.at[:, done], np_hbm.at[:, done], sem.at[1])]
     for copy in copies:
         copy.start()
-    out[...] = pr[:, rest] + dg(kept[...], u[...], NT).T
+    y = lax.axis_index("y")
+    out[...] = pr[:, rest] + product(kept, u, pl.ds(0, R - FIRST), tuple(rem(y + d, 4) for d in (1, 2, 3)))
     copies.append(pltpu.make_async_copy(out, np_hbm.at[:, rest], sem.at[2]))
     copies[-1].start()
     for copy in copies:
@@ -385,7 +392,7 @@
         name="ridge_step",
         in_specs=[pl.BlockSpec(memory_space=pltpu.SMEM)] + [hbm] * 5,
         out_specs=[vmem] * 4,
-        out_shape=[V((T, R), f32), V((T, R), f32), V((R - FIRST, B), bf16), V((T, B), bf16)],
+        out_shape=[V((T, R), f32), V((T, R), f32), V((R - FIRST, B), bf16), V((4, T, SLAB), bf16)],
         scratch_shapes=[
             V((FIRST, B), bf16), V((R, 2 * F), bf16), V((B, 2 * F), bf16), V((T, R), bf16),
             V((2, 128, B), f32), V((SLAB, B), bf16), V((SLAB, B), bf16), V((T, B), f32),

time: 76.1 us -> 74.1 us (0.974)
  Pallas kernels: 74.7 us -> 72.7 us
    pallas_call x1, Pallas kernels: 71.2 us -> 70 us  [body(): pl.pallas_call(kernel, name='ridge_step', in_specs=[pl.BlockSpec(memory_s...]
    pallas_call x1, Pallas kernels: 3.49 us -> 2.7 us  [body(): pl.pallas_call(finish, name='finish', in_specs=[vmem] * 4, out_specs=[hbm...]
where the time goes in v4:
time: 74.1 us; the launch traced here: 74 us
  Pallas kernels  72.7 us (98%)
  between operations  1.29 us (2%)
    pallas_call x1, Pallas kernels, body(): pl.pallas_call(kernel, name='ridge_step', in_specs=[pl.BlockSpec(memory_s...  70 us
    pallas_call x1, Pallas kernels, body(): pl.pallas_call(finish, name='finish', in_specs=[vmem] * 4, out_specs=[hbm...  2.7 us

profile of v4, /device:TPU:1, one launch (start us, length us, event | category | flops | bytes accessed | tf_op | source)
XLA Modules:
  0.0 74.0 jit_solution(2998467454453924876)
XLA Ops:
  1.3 70.0 %ridge_step.1 = (f32[64,8192]{1,0:T(8,128)S(1)}, f32[64,8192]{1,0:T(8,128)S(1)}, bf16[2048,2048]{1,0:T(8,128)(2,1)S(1)}, bf16[4,64,512]{2,1,0:T(8,128)(2,1)S(1)}) custom-call(s32[1]{0:T(128)S(6)} %copy.8.bid, bf16[8192,128]{1,0:T(8,128)(2,1)} %pts_hbm.1, f32[64,8192]{1,0:T(8,128)} %bitcast.5, f32[64,8192]{1,0:T(8,128)} %bitcast.6, f32[64,8192]{1,0:T(8,128)} %bitcast.7, ...), custom_call_target="tpu_custom_call" | custom-call | tf_op jit(solution)/shard_map/ridge_step/pallas_call | solution.py:390
  71.3 2.7 %finish.1 = (f32[64,8192]{1,0:T(8,128)}, f32[64,8192]{1,0:T(8,128)}) custom-call(f32[64,8192]{1,0:T(8,128)S(1)} %get-tuple-element.8.cf, f32[64,8192]{1,0:T(8,128)S(1)} %get-tuple-element.9.pr, bf16[2048,2048]{1,0:T(8,128)(2,1)S(1)} %get-tuple-element.10.kept, bf16[4,64,512]{2,1,0:T(8,128)(2,1)S(1)} %get-tuple-element.11.u), custom_call_target="tpu_custom_call" | custom-call | tf_op jit(solution)/shard_map/finish/pallas_call | solution.py:406
